TPU v7x, 32 devices: a whole 2x2x4 slice. The times are simulated.
32 devices in a mesh: expert: 4 (over y, x), tensor: 2 (over core), dp: 4 (over z).
Axes of the slice: x: 2, y: 2, z: 4, core: 2. Of those that a mesh axis runs over, the one named last changes fastest.
Arguments:
- tokens: bfloat16 [2048, 3072], P(('expert', 'dp'), 'tensor'), may hold values from -6 to 6
- experts_chosen: int32 [2048, 2], P(('expert', 'dp')), may hold values from 0 to 3, all different within a row; in each aligned block of 128 rows (0 to 127, 128 to 255, ...) at most 73 rows name the same one
- route_weights: float32 [2048, 2], P(('expert', 'dp')), may hold values from 0.1 to 1
- cotangent: bfloat16 [2048, 3072], P(('expert', 'dp'), 'tensor'), may hold values from -6 to 6
- gate_weight: bfloat16 [4, 3072, 8192], P('expert', 'dp', 'tensor'), may hold values from -0.15625 to 0.15625
- up_weight: bfloat16 [4, 3072, 8192], P('expert', 'dp', 'tensor'), may hold values from -0.15625 to 0.15625
- down_weight: bfloat16 [4, 8192, 3072], P('expert', 'tensor', 'dp'), may hold values from -0.09375 to 0.09375
Outputs:
- layer_output: bfloat16 [2048, 3072], P(('expert', 'dp'), 'tensor')
- token_grad: bfloat16 [2048, 3072], P(('expert', 'dp'), 'tensor')
- route_grad: float32 [2048, 2], P(('expert', 'dp'))
Inputs may be any that keep to these rules, and one draw needn't show every extreme that they name: `experts_chosen`: each row names 2 different experts. Among the 128 rows of one index of expert+dp no expert is named more than 73 times, and in some such block one expert is named exactly 73 times.
All inputs are finite; a program needn't handle non-finite values.
Results may differ from a plain program's by a relative error of at most 0.0072.
Values may be sent and summed in bfloat16 or wider, within the bound.
No kernel may reach another device: no remote copies, remote signals or barrier semaphores. Data moves between devices by JAX's collectives and lax.ppermute only.
A program may use at most 256 MiB of HBM per device.

v0:
```python
import jax
import jax.numpy as jnp
from jax import lax
from jax.sharding import PartitionSpec as P


def slot_table(experts_chosen, num_experts, cap_rows):
    flat_ids = experts_chosen.reshape(-1)
    expert_hot = (flat_ids[:, None] == jnp.arange(num_experts, dtype=jnp.int32)[None, :]).astype(
        jnp.int32
    )
    earlier = jnp.cumsum(expert_hot, axis=0) - expert_hot
    rank_slot = jnp.sum(earlier * expert_hot, axis=1)
    target = flat_ids * cap_rows + rank_slot
    all_slots = jnp.arange(num_experts * cap_rows, dtype=jnp.int32)
    return (target[:, None] == all_slots[None, :]).astype(jnp.bfloat16)


def to_slots(slot_onehot, pair_rows, num_experts, cap_rows):
    packed = jnp.einsum("ps,pd->sd", slot_onehot, pair_rows, preferred_element_type=jnp.float32)
    return packed.astype(jnp.bfloat16).reshape(num_experts, cap_rows, pair_rows.shape[1])


def from_slots(slot_onehot, returned):
    flat_back = returned.reshape(-1, returned.shape[2])
    return jnp.dot(slot_onehot, flat_back, preferred_element_type=jnp.float32)


def as_blocks(summed, num_experts, cap_rows):
    return summed.astype(jnp.bfloat16).reshape(num_experts, cap_rows, summed.shape[1])


def local(tokens, experts_chosen, route_weights, cotangent, gate_weight, up_weight, down_weight):
    tok_rows, feat_cols = tokens.shape
    top_count = experts_chosen.shape[1]
    num_experts = lax.axis_size("expert")
    cap_rows = min(tok_rows, 9 * tok_rows * top_count // (8 * num_experts) + 1)
    slot_onehot = slot_table(experts_chosen, num_experts, cap_rows)
    pair_weights = route_weights.reshape(-1, 1)
    token_pairs = jnp.repeat(tokens, top_count, axis=0)
    grad_pairs = (
        jnp.repeat(cotangent, top_count, axis=0).astype(jnp.float32) * pair_weights
    ).astype(jnp.bfloat16)
    token_send = to_slots(slot_onehot, token_pairs, num_experts, cap_rows)
    grad_send = to_slots(slot_onehot, grad_pairs, num_experts, cap_rows)
    token_recv = lax.all_to_all(token_send, "expert", split_axis=0, concat_axis=0, tiled=True)
    token_full = lax.all_gather(token_recv, "tensor", axis=2, tiled=True)
    model_cols = token_full.shape[2]
    token_rows = token_full.reshape(-1, model_cols)
    gate_all, up_all = (
        lax.all_gather(gate_weight, "dp", axis=1, tiled=True),
        lax.all_gather(up_weight, "dp", axis=1, tiled=True),
    )
    gate_pre = jnp.dot(token_rows, gate_all[0], preferred_element_type=jnp.float32)
    up_pre = jnp.dot(token_rows, up_all[0], preferred_element_type=jnp.float32)
    hidden = (jax.nn.silu(gate_pre) * up_pre).astype(jnp.bfloat16)
    down_all = lax.all_gather(down_weight, "dp", axis=2, tiled=True)
    out_part = jnp.dot(hidden, down_all[0], preferred_element_type=jnp.float32)
    out_sum = lax.psum_scatter(
        out_part.astype(jnp.bfloat16), "tensor", scatter_dimension=1, tiled=True
    ).astype(jnp.float32)
    out_back = lax.all_to_all(
        as_blocks(out_sum, num_experts, cap_rows), "expert", split_axis=0, concat_axis=0, tiled=True
    )
    grad_recv = lax.all_to_all(grad_send, "expert", split_axis=0, concat_axis=0, tiled=True)
    grad_full = lax.all_gather(grad_recv, "tensor", axis=2, tiled=True)
    grad_rows_all = grad_full.reshape(-1, model_cols)
    contract = (((1,), (1,)), ((), ()))
    hidden_grad = lax.dot_general(
        grad_rows_all, down_all[0], contract, preferred_element_type=jnp.float32
    )
    sigmoid_gate = jax.nn.sigmoid(gate_pre)
    up_grad = (hidden_grad * jax.nn.silu(gate_pre)).astype(jnp.bfloat16)
    gate_grad = (
        hidden_grad * up_pre * sigmoid_gate * (1.0 + gate_pre * (1.0 - sigmoid_gate))
    ).astype(jnp.bfloat16)
    in_part = lax.dot_general(gate_grad, gate_all[0], contract, preferred_element_type=jnp.float32)
    in_part = in_part + lax.dot_general(
        up_grad, up_all[0], contract, preferred_element_type=jnp.float32
    )
    in_sum = lax.psum_scatter(
        in_part.astype(jnp.bfloat16), "tensor", scatter_dimension=1, tiled=True
    ).astype(jnp.float32)
    in_back = lax.all_to_all(
        as_blocks(in_sum, num_experts, cap_rows), "expert", split_axis=0, concat_axis=0, tiled=True
    )
    out_pairs = from_slots(slot_onehot, out_back).reshape(tok_rows, top_count, feat_cols)
    in_pairs = from_slots(slot_onehot, in_back).reshape(tok_rows, top_count, feat_cols)
    layer_output = jnp.sum(route_weights[:, :, None] * out_pairs, axis=1).astype(jnp.bfloat16)
    token_grad = jnp.sum(in_pairs, axis=1).astype(jnp.bfloat16)
    local_dots = jnp.sum(cotangent.astype(jnp.float32)[:, None, :] * out_pairs, axis=2)
    route_grad = lax.psum(local_dots, "tensor")
    return (layer_output, token_grad, route_grad)


def solution(mesh):
    in_specs = (
        P(("expert", "dp"), "tensor"),
        P(("expert", "dp"), None),
        P(("expert", "dp"), None),
        P(("expert", "dp"), "tensor"),
        P("expert", "dp", "tensor"),
        P("expert", "dp", "tensor"),
        P("expert", "tensor", "dp"),
    )
    out_specs = (
        P(("expert", "dp"), "tensor"),
        P(("expert", "dp"), "tensor"),
        P(("expert", "dp"), None),
    )
    return jax.shard_map(local, mesh=mesh, in_specs=in_specs, out_specs=out_specs, check_vma=False)
```

profile of v0, /device:TPU:0, one launch (start us, length us, event | category | flops | bytes accessed | tf_op | source)
XLA Modules:
  0.0 1455.3 jit_solution(10602917999644850191)
XLA Ops:
  8.3 1.4 broadcast_in_dim.4
  12.5 18.7 %all_to_all.20 = bf16[4,73,1536]{2,1,0:T(8,128)(2,1)} all-to-all(bf16[4,73,1536]{2,1,0:T(8,128)(2,1)S(1)} %reshape.107), channel_id=1, replica_groups=mesh['expert'=4,'tensor'=2,'dp'=4] {'expert'}, dimensions={0} | all-to-all | bytes 1794048 | tf_op jit(solution)/shard_map/all_to_all | solution.py:46
  33.8 15.7 %all_to_all.21 = bf16[4,73,1536]{2,1,0:T(8,128)(2,1)} all-to-all(bf16[4,73,1536]{2,1,0:T(8,128)(2,1)S(1)} %reshape.111), channel_id=1, replica_groups=mesh['expert'=4,'tensor'=2,'dp'=4] {'expert'}, dimensions={0} | all-to-all | bytes 1794048 | tf_op jit(solution)/shard_map/all_to_all | solution.py:65
  51.7 2.0 reshape.108
  53.7 5.9 all-gather.14.cloned.1.call-done
  59.6 3.3 reshape.112
  62.9 424.7 %all-gather.10.cloned.1.call-done = bf16[1,3072,4096]{2,1,0:T(8,128)(2,1)} async-done(((bf16[1,768,4096]{2,1,0:T(8,128)(2,1)}), bf16[1,3072,4096]{2,1,0:T(8,128)(2,1)}) %all-gather.10.cloned.1.call-update) | async-done | bytes 25165840 | tf_op jit(solution)/shard_map/all_gather | solution.py:52
  487.6 16.4 %fusion.6 = f32[292,4096]{1,0:T(8,128)} fusion(bf16[292,3072]{1,0:T(8,128)(2,1)S(1)} %reshape.108, bf16[1,3072,4096]{2,1,0:T(8,128)(2,1)} %all-gather.10.cloned.1.call-done), kind=kOutput, calls=%fused_computation.6 | convolution fusion | flops 7348420608 | bytes 31744000 | tf_op jit(solution)/shard_map/dot_general | solution.py:55
  504.0 408.4 %all-gather.8.cloned.1.call-done = bf16[1,3072,4096]{2,1,0:T(8,128)(2,1)} async-done(((bf16[1,768,4096]{2,1,0:T(8,128)(2,1)}), bf16[1,3072,4096]{2,1,0:T(8,128)(2,1)}) %all-gather.8.cloned.1.call-update) | async-done | bytes 25165840 | tf_op jit(solution)/shard_map/all_gather | solution.py:51
  912.4 16.3 %fusion.10 = f32[292,4096]{1,0:T(8,128)} fusion(bf16[292,3072]{1,0:T(8,128)(2,1)S(1)} %reshape.108, bf16[1,3072,4096]{2,1,0:T(8,128)(2,1)} %all-gather.8.cloned.1.call-done), kind=kOutput, calls=%fused_computation.10 | convolution fusion | flops 7348420608 | bytes 31744000 | tf_op jit(solution)/shard_map/dot_general | solution.py:54
  928.8 408.5 %all-gather.12.cloned.1.call-done = bf16[1,4096,3072]{2,1,0:T(8,128)(2,1)} async-done(((bf16[1,4096,768]{2,1,0:T(8,128)(2,1)}), bf16[1,4096,3072]{2,1,0:T(8,128)(2,1)}) %all-gather.12.cloned.1.call-update) | async-done | bytes 25165840 | tf_op jit(solution)/shard_map/all_gather | solution.py:57
  1337.3 14.5 fusion
  1351.7 16.7 %fusion.4 = f32[292,3072]{1,0:T(8,128)} fusion(bf16[1,3072,4096]{2,1,0:T(8,128)(2,1)} %all-gather.10.cloned.1.call-done, f32[292,4096]{1,0:T(8,128)} %fusion, f32[292,4096]{1,0:T(8,128)} %fusion.10), kind=kOutput, calls=%fused_computation.4 | convolution fusion | flops 7355596800 | bytes 38322176 | tf_op jit(solution)/shard_map/dot_general | solution.py:78
  1368.5 21.3 %fusion.16 = bf16[292,3072]{1,0:T(8,128)(2,1)} fusion(f32[292,3072]{1,0:T(8,128)} %fusion.4, bf16[1,3072,4096]{2,1,0:T(8,128)(2,1)} %all-gather.8.cloned.1.call-done, f32[292,4096]{1,0:T(8,128)} %fusion.10, f32[292,4096]{1,0:T(8,128)} %fusion, f32[292,4096]{1,0:T(8,128)} %fusion.6), kind=kOutput, calls=%fused_computation.18 | convolution fusion | flops 7362174976 | bytes 44900352 | tf_op jit(solution)/shard_map/dot_general | solution.py:77
  1389.9 17.2 %fusion.19 = bf16[292,3072]{1,0:T(8,128)(2,1)} fusion(bf16[1,4096,3072]{2,1,0:T(8,128)(2,1)} %all-gather.12.cloned.1.call-done, f32[292,4096]{1,0:T(8,128)} %fusion.6, f32[292,4096]{1,0:T(8,128)} %fusion.10), kind=kOutput, calls=%fused_computation.19 | convolution fusion | flops 7356493824 | bytes 36528128 | tf_op jit(solution)/shard_map/dot_general | solution.py:58
  1407.1 2.4 reshape.113
  1409.5 3.6 all-to-all-start.3
  1413.2 1.5 reduce-scatter.3.cloned.1.call-done
  1414.7 2.4 reshape.109
  1417.1 9.3 all-to-all-done.3
  1426.5 3.5 all-to-all-start.1
  1432.8 9.6 all-to-all-done.1
  1442.7 2.7 multiply_reduce_fusion
  1445.4 3.0 psum.7
  (51 shorter events, 11.7 us)
Async XLA Ops:
  7.2 24.1 %copy-start = (bf16[128,1536]{1,0:T(8,128)(2,1)S(1)}, bf16[128,1536]{1,0:T(8,128)(2,1)}, u32[]{:S(2)}) copy-start(bf16[128,1536]{1,0:T(8,128)(2,1)} %param.10) | copy-start | bytes 1179652
  7.2 44.5 %all-gather.6.cloned.1.call-start = ((), (), s32[]{:S(2)}) async-start(), calls=%async_computation.6 | async-start | bytes 2949120 | tf_op jit(solution)/shard_map/all_gather | solution.py:47
  12.2 20.5 %copy-start.2 = (f32[128,2]{0,1:T(2,128)S(1)}, f32[128,2]{0,1:T(2,128)}, u32[]{:S(2)}) copy-start(f32[128,2]{0,1:T(2,128)} %param.9) | copy-start | bytes 3076
  31.2 28.4 %all-gather.14.cloned.1.call-start = ((), (), s32[]{:S(2)}) async-start(), calls=%async_computation.11 | async-start | bytes 2949120 | tf_op jit(solution)/shard_map/all_gather | solution.py:66
  49.5 438.1 %all-gather.10.cloned.1.call-start = ((), (), s32[]{:S(2)}) async-start(), calls=%async_computation.8 | async-start | bytes 31457280 | tf_op jit(solution)/shard_map/all_gather | solution.py:52
  50.3 862.2 %all-gather.8.cloned.1.call-start = ((), (), s32[]{:S(2)}) async-start(), calls=%async_computation.7 | async-start | bytes 31457280 | tf_op jit(solution)/shard_map/all_gather | solution.py:51
  50.9 1286.4 %all-gather.12.cloned.1.call-start = ((), (), s32[]{:S(2)}) async-start(), calls=%async_computation.9 | async-start | bytes 31457280 | tf_op jit(solution)/shard_map/all_gather | solution.py:57
  51.5 1355.7 %reduce-scatter.5.cloned.1.call-start = ((), (), s32[]{:S(2)}) async-start(), calls=%async_computation.12 | async-start | bytes 2727936 | tf_op jit(solution)/shard_map/reduce_scatter | solution.py:81
  1389.8 24.9 %reduce-scatter.3.cloned.1.call-start = ((), (), s32[]{:S(2)}) async-start(), calls=%async_computation.10 | async-start | bytes 2727936 | tf_op jit(solution)/shard_map/reduce_scatter | solution.py:59
  1407.1 24.1 %copy-start.1 = (s32[128,2]{0,1:T(2,128)S(1)}, s32[128,2]{0,1:T(2,128)}, u32[]{:S(2)}) copy-start(s32[128,2]{0,1:T(2,128)} %param.8) | copy-start | bytes 3076
  1409.5 16.9 %all-to-all-start.3 = ((bf16[4,73,1536]{2,1,0:T(8,128)(2,1)}), bf16[4,73,1536]{2,1,0:T(8,128)(2,1)S(1)}, u32[]{:S(2)}, u32[]{:S(2)}) async-start(bf16[4,73,1536]{2,1,0:T(8,128)(2,1)} %reshape.113), calls=%async_computation.5 | async-start | bytes 1966080 | tf_op jit(solution)/shard_map/all_to_all | solution.py:84
  1426.5 16.0 %all-to-all-start.1 = ((bf16[4,73,1536]{2,1,0:T(8,128)(2,1)}), bf16[4,73,1536]{2,1,0:T(8,128)(2,1)S(1)}, u32[]{:S(2)}, u32[]{:S(2)}) async-start(bf16[4,73,1536]{2,1,0:T(8,128)(2,1)} %reshape.109), calls=%async_computation.2 | async-start | bytes 1966080 | tf_op jit(solution)/shard_map/all_to_all | solution.py:62
Sparse Core Ops, SparseCore 0:
  31.3 9.9 all-gather.5
  49.7 9.9 all-gather.13
  61.2 426.3 all-gather.9
  489.0 423.3 all-gather.7
  913.9 423.3 all-gather.11
  1389.9 7.5 reduce-scatter.4
  1407.2 7.4 reduce-scatter.2
where the time goes:
time: 1460 us
  waiting for transfers between devices  1270 us (87%)
  matrix products  108 us (7%)
  blocking collectives  37.4 us (3%)
  local copies, waits for them, and re-layouts  16.2 us (1%)
    all_gather x1, waiting for transfers between devices, local(): lax.all_gather(up_weight, 'dp', axis=1, tiled=True)  425 us
    all_gather x1, waiting for transfers between devices, local(): down_all = lax.all_gather(down_weight, 'dp', axis=2, tiled=True)  408 us
    all_gather x1, waiting for transfers between devices, local(): lax.all_gather(gate_weight, 'dp', axis=1, tiled=True)  408 us
  transfers between devices with their start and end apart: 9, of which 7 were waited for; matrix products, arithmetic and copies ran while one was open for 4% of the time, Pallas kernels for 0%

commit v1 on v0

--- a/solution.py
+++ b/solution.py
@@ -54,7 +54,12 @@
     gate_pre = jnp.dot(token_rows, gate_all[0], preferred_element_type=jnp.float32)
     up_pre = jnp.dot(token_rows, up_all[0], preferred_element_type=jnp.float32)
     hidden = (jax.nn.silu(gate_pre) * up_pre).astype(jnp.bfloat16)
-    down_all = lax.all_gather(down_weight, "dp", axis=2, tiled=True)
+    ring = [down_weight]
+    for hop in range(3):
+        ring.append(lax.ppermute(ring[-1], "dp", [(dev, (dev + 1) % 4) for dev in range(4)]))
+    down_all = jnp.roll(
+        jnp.concatenate(ring[::-1], axis=2), (lax.axis_index("dp") + 1) * ring[0].shape[2], axis=2
+    )
     out_part = jnp.dot(hidden, down_all[0], preferred_element_type=jnp.float32)
     out_sum = lax.psum_scatter(
         out_part.astype(jnp.bfloat16), "tensor", scatter_dimension=1, tiled=True

time: 1460 us -> 1390 us (0.952)
  waiting for transfers between devices: 1270 us -> 992 us
  starting transfers between devices: 7.58 us -> 177 us
  local copies, waits for them, and re-layouts: 16.2 us -> 58 us
    ppermute x0 -> x3, waiting for transfers between devices: none -> 753 us  [local(): lax.ppermute(ring[-1], 'dp', [(dev, (dev + 1) % 4) for dev in range(4)])]
    all_gather x1, waiting for transfers between devices: 425 us -> 0.01 us  [local(): lax.all_gather(up_weight, 'dp', axis=1, tiled=True)]
    all_gather x1 -> x0, waiting for transfers between devices: 408 us -> none  [local(): down_all = lax.all_gather(down_weight, 'dp', axis=2, tiled=True)]
    all_gather x1, waiting for transfers between devices: 408 us -> 217 us  [local(): lax.all_gather(gate_weight, 'dp', axis=1, tiled=True)]
    ppermute x0 -> x3, starting transfers between devices: none -> 169 us  [local(): lax.ppermute(ring[-1], 'dp', [(dev, (dev + 1) % 4) for dev in range(4)])]
    unnamed x8 -> x35, local copies, waits for them, and re-layouts: 0.96 us -> 38.3 us
  transfers between devices with their start and end apart: 9 -> 11, of which waited for: 7 -> 7; matrix products, arithmetic and copies ran while one was open for 4% -> 8% of each run, Pallas kernels for 0% -> 0%
where the time goes in v1:
time: 1390 us
  waiting for transfers between devices  992 us (71%)
  starting transfers between devices  177 us (13%)
  matrix products  109 us (8%)
  local copies, waits for them, and re-layouts  58 us (4%)
  blocking collectives  37.3 us (3%)
  between operations  14.3 us (1%)
    ppermute x3, waiting for transfers between devices, local(): lax.ppermute(ring[-1], 'dp', [(dev, (dev + 1) % 4) for dev in range(4)])  753 us
    all_gather x1, waiting for transfers between devices, local(): lax.all_gather(gate_weight, 'dp', axis=1, tiled=True)  217 us
    ppermute x3, starting transfers between devices, local(): lax.ppermute(ring[-1], 'dp', [(dev, (dev + 1) % 4) for dev in range(4)])  169 us
    unnamed x35, local copies, waits for them, and re-layouts  38.3 us
  transfers between devices with their start and end apart: 11, of which 7 were waited for; matrix products, arithmetic and copies ran while one was open for 8% of the time, Pallas kernels for 0%

profile of v1, /device:TPU:0, one launch (start us, length us, event | category | flops | bytes accessed | tf_op | source)
XLA Modules:
  0.0 1389.9 jit_solution(2359378871206408651)
XLA Ops:
  13.1 18.7 %all_to_all.20 = bf16[4,73,1536]{2,1,0:T(8,128)(2,1)} all-to-all(bf16[4,73,1536]{2,1,0:T(8,128)(2,1)S(1)} %reshape.107), channel_id=1, replica_groups=mesh['expert'=4,'tensor'=2,'dp'=4] {'expert'}, dimensions={0} | all-to-all | bytes 1794048 | tf_op jit(solution)/shard_map/all_to_all | solution.py:46
  34.4 15.6 %all_to_all.21 = bf16[4,73,1536]{2,1,0:T(8,128)(2,1)} all-to-all(bf16[4,73,1536]{2,1,0:T(8,128)(2,1)S(1)} %reshape.111), channel_id=1, replica_groups=mesh['expert'=4,'tensor'=2,'dp'=4] {'expert'}, dimensions={0} | all-to-all | bytes 1794048 | tf_op jit(solution)/shard_map/all_to_all | solution.py:70
  53.1 244.2 %collective-permute-done = bf16[1,4096,768]{2,1,0:T(8,128)(2,1)S(1)} collective-permute-done((bf16[1,4096,768]{2,1,0:T(8,128)(2,1)}, bf16[1,4096,768]{2,1,0:T(8,128)(2,1)S(1)}, u32[]{:S(2)}, u32[]{:S(2)}) %collective-permute-start) | collective-permute-done | bytes 6291488 | tf_op jit(solution)/shard_map/ppermute | solution.py:59
  299.8 120.0 %collective-permute-start.1 = (bf16[1,4096,768]{2,1,0:T(8,128)(2,1)S(1)}, bf16[1,4096,768]{2,1,0:T(8,128)(2,1)}, u32[]{:S(2)}, u32[]{:S(2)}) collective-permute-start(bf16[1,4096,768]{2,1,0:T(8,128)(2,1)S(1)} %collective-permute-done), channel_id=1, source_target_pairs={{0,1},{1,2},{2,3},{3,0},{4,5},{5,6},{6,7},{7,4},{8,9},{9,10},{10,1... | collective-permute-start | bytes 18874376 | tf_op jit(solution)/shard_map/ppermute | solution.py:59
  419.9 260.1 %collective-permute-done.1 = bf16[1,4096,768]{2,1,0:T(8,128)(2,1)} collective-permute-done((bf16[1,4096,768]{2,1,0:T(8,128)(2,1)S(1)}, bf16[1,4096,768]{2,1,0:T(8,128)(2,1)}, u32[]{:S(2)}, u32[]{:S(2)}) %collective-permute-start.1) | collective-permute-done | bytes 6291488 | tf_op jit(solution)/shard_map/ppermute | solution.py:59
  680.0 47.8 %collective-permute-start.2 = (bf16[1,4096,768]{2,1,0:T(8,128)(2,1)}, bf16[1,4096,768]{2,1,0:T(8,128)(2,1)}, u32[]{:S(2)}, u32[]{:S(2)}) collective-permute-start(bf16[1,4096,768]{2,1,0:T(8,128)(2,1)} %collective-permute-done.1), channel_id=1, source_target_pairs={{0,1},{1,2},{2,3},{3,0},{4,5},{5,6},{6,7},{7,4},{8,9},{9,10},{10,1... | collective-permute-start | bytes 18874376 | tf_op jit(solution)/shard_map/ppermute | solution.py:59
  731.0 3.4 reshape.112
  734.4 248.7 %collective-permute-done.2 = bf16[1,4096,768]{2,1,0:T(8,128)(2,1)} collective-permute-done((bf16[1,4096,768]{2,1,0:T(8,128)(2,1)}, bf16[1,4096,768]{2,1,0:T(8,128)(2,1)}, u32[]{:S(2)}, u32[]{:S(2)}) %collective-permute-start.2) | collective-permute-done | bytes 6291488 | tf_op jit(solution)/shard_map/ppermute | solution.py:59
  983.1 6.1 constant_dynamic-update-slice_fusion.7
  989.3 6.3 constant_dynamic-update-slice_fusion.6
  998.6 3.3 constant_dynamic-update-slice_fusion.4
  1001.9 6.2 constant_dynamic-update-slice_fusion.3
  1008.2 5.9 constant_dynamic-update-slice_fusion.2
  1020.4 16.1 %fusion = f32[292,4096]{1,0:T(8,128)} fusion(bf16[292,3072]{1,0:T(8,128)(2,1)} %reshape.112, bf16[1,4096,6144]{2,1,0:T(8,128)(2,1)} %constant_dynamic-update-slice_fusion, s32[]{:T(128)S(6)} %select_n.14), kind=kOutput, calls=%fused_computation | convolution fusion | flops 7348420608 | bytes 31768580 | tf_op jit(solution)/shard_map/dot_general | solution.py:74
  1036.5 14.4 %fusion.6 = f32[292,4096]{1,0:T(8,128)} fusion(bf16[292,3072]{1,0:T(8,128)(2,1)S(1)} %copy-done.1, bf16[1,3072,4096]{2,1,0:T(8,128)(2,1)} %all-gather.9.cloned.1.call-done), kind=kOutput, calls=%fused_computation.6 | convolution fusion | flops 7348420608 | bytes 31744000 | tf_op jit(solution)/shard_map/dot_general | solution.py:55
  1050.9 216.8 %all-gather.7.cloned.1.call-done = bf16[1,3072,4096]{2,1,0:T(8,128)(2,1)} async-done(((bf16[1,768,4096]{2,1,0:T(8,128)(2,1)}), bf16[1,3072,4096]{2,1,0:T(8,128)(2,1)}) %all-gather.7.cloned.1.call-update) | async-done | bytes 25165840 | tf_op jit(solution)/shard_map/all_gather | solution.py:51
  1267.8 14.4 %fusion.10 = f32[292,4096]{1,0:T(8,128)} fusion(bf16[292,3072]{1,0:T(8,128)(2,1)S(1)} %copy-done.1, bf16[1,3072,4096]{2,1,0:T(8,128)(2,1)} %all-gather.7.cloned.1.call-done), kind=kOutput, calls=%fused_computation.10 | convolution fusion | flops 7348420608 | bytes 31744000 | tf_op jit(solution)/shard_map/dot_general | solution.py:54
  1282.2 16.7 %fusion.4 = f32[292,3072]{1,0:T(8,128)} fusion(bf16[1,3072,4096]{2,1,0:T(8,128)(2,1)} %all-gather.9.cloned.1.call-done, f32[292,4096]{1,0:T(8,128)} %fusion, f32[292,4096]{1,0:T(8,128)} %fusion.10), kind=kOutput, calls=%fused_computation.4 | convolution fusion | flops 7355596800 | bytes 38322176 | tf_op jit(solution)/shard_map/dot_general | solution.py:83
  1298.8 21.3 %fusion.18 = bf16[292,3072]{1,0:T(8,128)(2,1)} fusion(f32[292,3072]{1,0:T(8,128)} %fusion.4, bf16[1,3072,4096]{2,1,0:T(8,128)(2,1)} %all-gather.7.cloned.1.call-done, f32[292,4096]{1,0:T(8,128)} %fusion.10, f32[292,4096]{1,0:T(8,128)} %fusion, f32[292,4096]{1,0:T(8,128)} %fusion.6), kind=kOutput, calls=%fused_computation.20 | convolution fusion | flops 7362174976 | bytes 44900352 | tf_op jit(solution)/shard_map/dot_general | solution.py:82
  1320.2 21.3 %fusion.21 = bf16[292,3072]{1,0:T(8,128)(2,1)} fusion(bf16[1,4096,6144]{2,1,0:T(8,128)(2,1)} %constant_dynamic-update-slice_fusion, s32[]{:T(128)S(6)} %select_n.14, f32[292,4096]{1,0:T(8,128)} %fusion.6, f32[292,4096]{1,0:T(8,128)} %fusion.10), kind=kOutput, calls=%fused_computation.21 | convolution fusion | flops 7356493824 | bytes 36659204 | tf_op jit(solution)/shard_map/dot_general | solution.py:63
  1344.1 3.5 all-to-all-start.3
  1350.6 10.4 all-to-all-done.3
  1361.0 3.5 all-to-all-start.1
  1367.4 9.7 all-to-all-done.1
  (84 shorter events, 41.0 us)
Async XLA Ops:
  7.2 24.7 %copy-start.2 = (bf16[128,1536]{1,0:T(8,128)(2,1)S(1)}, bf16[128,1536]{1,0:T(8,128)(2,1)}, u32[]{:S(2)}) copy-start(bf16[128,1536]{1,0:T(8,128)(2,1)} %param.10) | copy-start | bytes 1179652
  7.2 720.6 %all-gather.5.cloned.1.call-start = ((), (), s32[]{:S(2)}) async-start(), calls=%async_computation.6 | async-start | bytes 2949120 | tf_op jit(solution)/shard_map/all_gather | solution.py:47
  11.7 0.6 copy-start.4
  12.8 20.5 %copy-start.7 = (f32[128,2]{0,1:T(2,128)S(1)}, f32[128,2]{0,1:T(2,128)}, u32[]{:S(2)}) copy-start(f32[128,2]{0,1:T(2,128)} %param.9) | copy-start | bytes 3076
  31.8 699.3 %all-gather.11.cloned.1.call-start = ((), (), s32[]{:S(2)}) async-start(), calls=%async_computation.10 | async-start | bytes 2949120 | tf_op jit(solution)/shard_map/all_gather | solution.py:71
  50.1 986.4 %all-gather.9.cloned.1.call-start = ((), (), s32[]{:S(2)}) async-start(), calls=%async_computation.8 | async-start | bytes 31457280 | tf_op jit(solution)/shard_map/all_gather | solution.py:52
  50.8 1217.0 %all-gather.7.cloned.1.call-start = ((), (), s32[]{:S(2)}) async-start(), calls=%async_computation.7 | async-start | bytes 31457280 | tf_op jit(solution)/shard_map/all_gather | solution.py:51
  51.4 1290.2 %reduce-scatter.5.cloned.1.call-start = ((), (), s32[]{:S(2)}) async-start(), calls=%async_computation.11 | async-start | bytes 2727936 | tf_op jit(solution)/shard_map/reduce_scatter | solution.py:86
  51.4 245.9 %collective-permute-start = (bf16[1,4096,768]{2,1,0:T(8,128)(2,1)}, bf16[1,4096,768]{2,1,0:T(8,128)(2,1)S(1)}, u32[]{:S(2)}, u32[]{:S(2)}) collective-permute-start(bf16[1,4096,768]{2,1,0:T(8,128)(2,1)} %param.13), channel_id=1, source_target_pairs={{0,1},{1,2},{2,3},{3,0},{4,5},{5,6},{6,7},{7,4},{8,9},{9,10},{10,1... | collective-permute-start | bytes 18874376 | tf_op jit(solution)/shard_map/ppermute | solution.py:59
  297.3 2.6 copy-start
  299.8 380.2 %collective-permute-start.1 = (bf16[1,4096,768]{2,1,0:T(8,128)(2,1)S(1)}, bf16[1,4096,768]{2,1,0:T(8,128)(2,1)}, u32[]{:S(2)}, u32[]{:S(2)}) collective-permute-start(bf16[1,4096,768]{2,1,0:T(8,128)(2,1)S(1)} %collective-permute-done), channel_id=1, source_target_pairs={{0,1},{1,2},{2,3},{3,0},{4,5},{5,6},{6,7},{7,4},{8,9},{9,10},{10,1... | collective-permute-start | bytes 18874376 | tf_op jit(solution)/shard_map/ppermute | solution.py:59
  680.0 303.1 %collective-permute-start.2 = (bf16[1,4096,768]{2,1,0:T(8,128)(2,1)}, bf16[1,4096,768]{2,1,0:T(8,128)(2,1)}, u32[]{:S(2)}, u32[]{:S(2)}) collective-permute-start(bf16[1,4096,768]{2,1,0:T(8,128)(2,1)} %collective-permute-done.1), channel_id=1, source_target_pairs={{0,1},{1,2},{2,3},{3,0},{4,5},{5,6},{6,7},{7,4},{8,9},{9,10},{10,1... | collective-permute-start | bytes 18874376 | tf_op jit(solution)/shard_map/ppermute | solution.py:59
  731.0 264.5 %slice-start.2 = ((s8[6291456]{0:T(1024)(128)(4,1)}), s8[2097152]{0:T(1024)(128)(4,1)S(1)}, s32[]{:S(2)}) async-start(s8[6291456]{0:T(1024)(128)(4,1)} %bitcast.54), calls=%async_computation.14 | async-start | bytes 4194304
  734.4 261.1 %slice-start.3 = ((s8[6291456]{0:T(1024)(128)(4,1)}), s8[4194304]{0:T(1024)(128)(4,1)S(1)}, s32[]{:S(2)}) async-start(s8[6291456]{0:T(1024)(128)(4,1)} %bitcast.54), calls=%async_computation.15 | async-start | bytes 8388608
  989.2 9.4 slice-start
  995.6 3.1 slice-start.1
  1020.4 16.1 %copy-start.1 = (bf16[292,3072]{1,0:T(8,128)(2,1)S(1)}, bf16[292,3072]{1,0:T(8,128)(2,1)}, u32[]{:S(2)}) copy-start(bf16[292,3072]{1,0:T(8,128)(2,1)} %reshape.108) | copy-start | bytes 5382148
  1320.2 28.0 %reduce-scatter.3.cloned.1.call-start = ((), (), s32[]{:S(2)}) async-start(), calls=%async_computation.9 | async-start | bytes 2727936 | tf_op jit(solution)/shard_map/reduce_scatter | solution.py:64
  1341.5 23.0 %copy-start.3 = (bf16[128,1536]{1,0:T(8,128)(2,1)S(1)}, bf16[128,1536]{1,0:T(8,128)(2,1)}, u32[]{:S(2)}) copy-start(bf16[128,1536]{1,0:T(8,128)(2,1)} %param.10) | copy-start | bytes 1179652
  1341.5 24.0 %copy-start.5 = (s32[256]{0:T(256)S(1)}, s32[256]{0:T(256)}, u32[]{:S(2)}) copy-start(s32[256]{0:T(256)} %copy-done.4) | copy-start | bytes 3076
  1341.6 24.2 %copy-start.6 = (s32[128,2]{0,1:T(2,128)S(1)}, s32[128,2]{0,1:T(2,128)}, u32[]{:S(2)}) copy-start(s32[128,2]{0,1:T(2,128)} %param.8) | copy-start | bytes 3076
  1344.1 17.0 %all-to-all-start.3 = ((bf16[4,73,1536]{2,1,0:T(8,128)(2,1)}), bf16[4,73,1536]{2,1,0:T(8,128)(2,1)S(1)}, u32[]{:S(2)}, u32[]{:S(2)}) async-start(bf16[4,73,1536]{2,1,0:T(8,128)(2,1)} %reshape.113), calls=%async_computation.5 | async-start | bytes 1966080 | tf_op jit(solution)/shard_map/all_to_all | solution.py:89
  1347.6 29.8 %copy-start.8 = (f32[128,2]{0,1:T(2,128)S(1)}, f32[128,2]{0,1:T(2,128)}, u32[]{:S(2)}) copy-start(f32[128,2]{0,1:T(2,128)} %param.9) | copy-start | bytes 3076
  1361.0 16.1 %all-to-all-start.1 = ((bf16[4,73,1536]{2,1,0:T(8,128)(2,1)}), bf16[4,73,1536]{2,1,0:T(8,128)(2,1)S(1)}, u32[]{:S(2)}, u32[]{:S(2)}) async-start(bf16[4,73,1536]{2,1,0:T(8,128)(2,1)} %reshape.109), calls=%async_computation.2 | async-start | bytes 1966080 | tf_op jit(solution)/shard_map/all_to_all | solution.py:67
Sparse Core Ops, SparseCore 0:
  31.9 9.9 all-gather.4
  50.2 9.9 all-gather.10
  61.7 667.5 all-gather.8
  730.8 536.9 all-gather.6
  1320.3 6.7 reduce-scatter.4
  1341.7 6.4 reduce-scatter.2
